TPU v7x, 32 devices: a whole 2x2x4 slice. The times are simulated.
32 devices in a mesh: dp: 8 (over z, x), tensor: 4 (over y, core).
Axes of the slice: x: 2, y: 2, z: 4, core: 2. Of those that a mesh axis runs over, the one named last changes fastest.
Arguments:
- inputs: bfloat16 [16, 1024, 1024], P('dp'), may hold values from -6 to 6
- segment_ids: int32 [16, 1024], P('dp'), may hold values from 0 to 7, never falling along the last dimension, each value on 1 to 512 neighbouring positions
- doc_offsets: int32 [16, 8], P('dp'), may hold values from 0 to 3071
- time_index: int32 [16], P('dp'), may hold values from 0 to 999
- w_qkv: bfloat16 [3, 1024, 1024], P(None, 'dp', 'tensor'), may hold values from -0.1875 to 0.1875
- w_out: bfloat16 [1024, 1024], P('tensor', 'dp'), may hold values from -0.75 to 0.75
- w_up: bfloat16 [1024, 4096], P('dp', 'tensor'), may hold values from -0.1875 to 0.1875
- w_down: bfloat16 [4096, 1024], P('tensor', 'dp'), may hold values from -0.09375 to 0.09375
- w_time: bfloat16 [256, 1024], P(None, 'dp'), may hold values from -0.375 to 0.375
- gain_attn: bfloat16 [1024], P('dp'), may hold values from 0.5 to 1.5
- gain_mlp: bfloat16 [1024], P('dp'), may hold values from 0.5 to 1.5
- cotangent: bfloat16 [16, 1024, 1024], P('dp'), may hold values from -6 to 6
Outputs:
- block_out: bfloat16 [16, 1024, 1024], P('dp', None, 'tensor')
- input_grad: float32 [16, 1024, 1024], P('dp', None, 'tensor')
- grad_qkv: float32 [3, 1024, 1024], P(None, 'dp', 'tensor')
- grad_out: float32 [1024, 1024], P('tensor', 'dp')
- grad_up: float32 [1024, 4096], P('dp', 'tensor')
- grad_down: float32 [4096, 1024], P('tensor', 'dp')
- grad_time: float32 [256, 1024], P(None, 'dp')
- grad_gain_attn: float32 [1024], P('dp')
- grad_gain_mlp: float32 [1024], P('dp')
Inputs may be any that keep to these rules, and one draw needn't show every extreme that they name: `segment_ids`: in each sequence the ids never fall, every id of 0 to 7 occurs, each document has 1 to 512 tokens and one has exactly 512.
All inputs are finite; a program needn't handle non-finite values.
Results may differ from a plain program's by a relative error of at most 0.022.
Values may be sent and summed in bfloat16 or wider, within the bound.
No kernel may reach another device: no remote copies, remote signals or barrier semaphores. Data moves between devices by JAX's collectives and lax.ppermute only.
A program may use at most 192 MiB of HBM per device.

v0:
```python
import math
import jax
import jax.numpy as jnp
from jax import lax
from jax.sharding import PartitionSpec as P

HEADS = 16
TEMB = 256
eps = 1e-05
masked = -1000000000.0
f32 = jnp.float32
bf16 = jnp.bfloat16


def sinusoid(values, width):
    half = width // 2
    freqs = jnp.exp(-math.log(10000.0) * jnp.arange(half, dtype=f32) / half)
    angles = values[..., None] * freqs
    return jnp.concatenate([jnp.sin(angles), jnp.cos(angles)], axis=-1)


def norm_parts(hidden):
    centre = jnp.mean(hidden, axis=-1, keepdims=True)
    centred = hidden - centre
    spread = jnp.mean(centred * centred, axis=-1, keepdims=True)
    inv = lax.rsqrt(spread + eps)
    return (centred * inv, inv)


def norm_back(unit, inv, gain, grad):
    scaled = grad * gain
    first = jnp.mean(scaled, axis=-1, keepdims=True)
    second = jnp.mean(scaled * unit, axis=-1, keepdims=True)
    return inv * (scaled - first - unit * second)


def positions(segs, offsets):
    seq_len = segs.shape[0]
    index = jnp.arange(seq_len, dtype=jnp.int32)
    member = segs[:, None] == jnp.arange(offsets.shape[0], dtype=jnp.int32)[None, :]
    starts = jnp.min(jnp.where(member, index[:, None], seq_len), axis=0)
    start_tok = jnp.sum(jnp.where(member, starts[None, :], 0), axis=1)
    offset_tok = jnp.sum(jnp.where(member, offsets[None, :], 0), axis=1)
    return offset_tok + index - start_tok


def attend(query, key, value, same, scale):
    scores = jnp.einsum("qhe,khe->hqk", query, key, preferred_element_type=f32) * scale
    scores = jnp.where(same[None], scores, masked)
    top = jnp.max(scores, axis=-1, keepdims=True)
    expo = jnp.exp(scores - top)
    denom = jnp.sum(expo, axis=-1, keepdims=True)
    probs = (expo / denom).astype(bf16)
    out = jnp.einsum("hqk,khe->qhe", probs, value, preferred_element_type=f32)
    return (out, top + jnp.log(denom))


def attend_back(query, key, value, same, scale, lse, d_mixed):
    scores = jnp.einsum("qhe,khe->hqk", query, key, preferred_element_type=f32) * scale
    scores = jnp.where(same[None], scores, masked)
    probs = jnp.exp(scores - lse)
    d_probs = jnp.einsum("qhe,khe->hqk", d_mixed, value, preferred_element_type=f32)
    d_value = jnp.einsum("hqk,qhe->khe", probs.astype(bf16), d_mixed, preferred_element_type=f32)
    delta = jnp.sum(probs * d_probs, axis=-1, keepdims=True)
    d_scores = (probs * (d_probs - delta)).astype(bf16)
    d_query = jnp.einsum("hqk,khe->qhe", d_scores, key, preferred_element_type=f32) * scale
    d_key = jnp.einsum("hqk,qhe->khe", d_scores, query, preferred_element_type=f32) * scale
    return (d_query, d_key, d_value)


def mm(left, right):
    return jnp.dot(left, right, preferred_element_type=f32)


def mm_rt(left, right):
    return jnp.einsum("ik,jk->ij", left, right, preferred_element_type=f32)


def mm_lt(left, right):
    return jnp.einsum("ki,kj->ij", left, right, preferred_element_type=f32)


class Ring:

    def __init__(self, n):
        self.n = n
        self.order = list(range(0, n, 2)) + list(range(n - 1, 0, -2))
        inverse = [self.order.index(i) for i in range(n)]
        self.me = lax.axis_index("dp")
        self.spot = jnp.array(inverse, jnp.int32)[self.me]
        self.table = jnp.array(self.order, jnp.int32)
        self.right = [(self.order[p], self.order[(p + 1) % n]) for p in range(n)]
        self.left = [(b, a) for a, b in self.right]

    def at(self, offset):
        return self.table[(self.spot + offset) % self.n]

    def gather(self, block):
        rows = block.shape[0]
        full = jnp.zeros((self.n * rows,) + block.shape[1:], block.dtype)
        full = lax.dynamic_update_slice_in_dim(full, block, self.me * rows, 0)
        from_left = from_right = block
        for hop in range(1, self.n // 2 + 1):
            from_left = lax.ppermute(from_left, "dp", self.right)
            if hop <= self.n - 1 - self.n // 2:
                from_right = lax.ppermute(from_right, "dp", self.left)
                full = lax.dynamic_update_slice_in_dim(full, from_right, self.at(hop) * rows, 0)
            full = lax.dynamic_update_slice_in_dim(full, from_left, self.at(-hop) * rows, 0)
        return full

    def scatter(self, full):
        rows = full.shape[0] // self.n

        def part(offset):
            return lax.dynamic_slice_in_dim(full, self.at(offset) * rows, rows, 0).astype(f32)

        total = part(0)
        for hops, way, sign in (
            (self.n // 2, self.right, 1),
            (self.n - 1 - self.n // 2, self.left, -1),
        ):
            run = part(sign * hops)
            for hop in range(1, hops + 1):
                run = lax.ppermute(run.astype(bf16), "dp", way).astype(f32)
                if hop < hops:
                    run = run + part(sign * (hops - hop))
            if hops:
                total = total + run
        return total


def swap(value, bit, n):
    return lax.ppermute(value, "tensor", [(i, i ^ bit) for i in range(n)])


def to_features(value, n):
    me = lax.axis_index("tensor")
    tokens, width = value.shape
    value = value.reshape(tokens, n, width // n)
    bit = 1
    while bit < n:
        value = value.reshape(tokens, -1, 2, width // n)
        mine = me // bit % 2
        keep = lax.dynamic_index_in_dim(value, mine, 2, keepdims=False)
        send = lax.dynamic_index_in_dim(value, 1 - mine, 2, keepdims=False)
        got = swap(send.astype(bf16), bit, n).astype(f32)
        if bit == 1:
            got = jnp.concatenate([got[tokens // 2 :], got[: tokens // 2]], axis=0)
        value = keep.astype(f32) + got
        bit *= 2
    return value.reshape(tokens, width // n)


def shards(
    inputs,
    segment_ids,
    doc_offsets,
    time_index,
    w_qkv,
    w_out,
    w_up,
    w_down,
    w_time,
    gain_attn,
    gain_mlp,
    cotangent,
):
    n_dp = lax.axis_size("dp")
    n_tensor = lax.axis_size("tensor")
    me_dp = lax.axis_index("dp")
    core = lax.axis_index("tensor") % 2
    chips = n_tensor // 2
    seqs_dev, seq_len, width = inputs.shape
    half = seq_len // 2
    shard = width // n_tensor
    head_size = width // HEADS
    heads_dev = shard // head_size
    scale = head_size ** (-0.5)
    hidden_dev = w_up.shape[1]
    ring = Ring(n_dp)
    w1_part = jnp.concatenate([w_qkv[0], w_qkv[1], w_qkv[2], w_out.T], axis=1)
    w1 = ring.gather(w1_part)
    w2_part = jnp.concatenate([w_up, w_down.T], axis=1)
    w2 = lax.all_gather(w2_part, "dp", axis=0, tiled=True)
    times = lax.all_gather(time_index, "dp", axis=0, tiled=True)
    temb = sinusoid(times.astype(f32), TEMB)
    cond_part = jnp.dot(temb, w_time.astype(f32), precision=lax.Precision.HIGHEST)
    small = jnp.concatenate(
        [cond_part, gain_attn.astype(f32)[None], gain_mlp.astype(f32)[None]], axis=0
    )
    small = lax.all_gather(small, "dp", axis=1, tiled=True)
    n_seqs = n_dp * seqs_dev
    cond = lax.dynamic_slice_in_dim(small, me_dp * seqs_dev, seqs_dev, 0)
    attn_g, mlp_g = (small[n_seqs], small[n_seqs + 1])

    def own_first(value):
        return jnp.roll(value, -core * half, axis=0)

    def exchange_core(value):
        return swap(value, 1, n_tensor)

    def sum_chips(value):
        bit = 2
        value = value.astype(f32)
        while bit < n_tensor:
            low = value.astype(bf16)
            value = low.astype(f32) + swap(low, bit, n_tensor).astype(f32)
            bit *= 2
        return value

    seqs = range(seqs_dev)
    cot = [own_first(cotangent[i]) for i in seqs]
    segs = [own_first(segment_ids[i]) for i in seqs]
    same = [s[:, None] == s[None, :] for s in segs]
    h0, unit0, inv0, n1 = ([], [], [], [])
    for i in seqs:
        place = own_first(positions(segment_ids[i], doc_offsets[i]))
        h = own_first(inputs[i]).astype(f32) + sinusoid(place.astype(f32), width) + cond[i][None]
        unit, inv = norm_parts(h)
        h0.append(h)
        unit0.append(unit)
        inv0.append(inv)
        n1.append((unit * attn_g).astype(bf16))
    query, key, value, mixed, lse = ([], [], [], [], [])
    h1, unit1, inv1, n2 = ([], [], [], [])
    for i in seqs:
        qkv = mm(n1[i], w1[:, : 3 * shard]).astype(bf16)
        heads = [
            qkv[:, c * shard : (c + 1) * shard].reshape(seq_len, heads_dev, head_size)
            for c in range(3)
        ]
        out, total = attend(*heads, same[i], scale)
        out = out.reshape(seq_len, shard).astype(bf16)
        send = mm_rt(out[half:], w1[:, 3 * shard :]).astype(bf16)
        keep = mm_rt(out[:half], w1[:, 3 * shard :]).astype(bf16)
        attn = sum_chips(keep.astype(f32) + exchange_core(send).astype(f32))
        h = h0[i][:half] + attn
        unit, inv = norm_parts(h)
        own = (unit * mlp_g).astype(bf16)
        query.append(heads[0])
        key.append(heads[1])
        value.append(heads[2])
        mixed.append(out)
        lse.append(total)
        h1.append(h)
        unit1.append(unit)
        inv1.append(inv)
        n2.append(jnp.concatenate([own, exchange_core(own)], axis=0))
    w_up_full, w_down_t = (w2[:, :hidden_dev], w2[:, hidden_dev:])
    active, d_hidden, d_h1, d_h1_low, block_out = ([], [], [], [], [])
    gain_mlp_sum = jnp.zeros((width,), f32)
    for i in seqs:
        hidden = mm(n2[i], w_up_full)
        d_active = mm(cot[i], w_down_t)
        erf = lax.erf(hidden * 0.5**0.5)
        cdf = 0.5 + 0.5 * erf
        active.append((hidden * cdf).astype(bf16))
        slope = cdf + hidden * jnp.exp(-0.5 * hidden * hidden) * (0.5 / math.pi) ** 0.5
        d_hidden.append((d_active * slope).astype(bf16))
        d_n2_send = mm_rt(d_hidden[i][half:], w_up_full).astype(bf16)
        d_n2_keep = mm_rt(d_hidden[i][:half], w_up_full).astype(bf16)
        d_n2 = sum_chips(d_n2_keep.astype(f32) + exchange_core(d_n2_send).astype(f32))
        gain_mlp_sum = gain_mlp_sum + jnp.sum(d_n2 * unit1[i], axis=0)
        d_h1.append(cot[i][:half].astype(f32) + norm_back(unit1[i], inv1[i], mlp_g, d_n2))
        low = d_h1[i].astype(bf16)
        d_h1_low.append(jnp.concatenate([low, exchange_core(low)], axis=0))
        term = mm_rt(active[i], w_down_t)
        term = jnp.concatenate([term[:half] + h1[i] * (1.0 / chips), term[half:]], axis=0)
        block_out.append(to_features(term.astype(bf16), n_tensor).astype(bf16))
    cot_all = jnp.concatenate(cot, axis=0)
    grad2 = jnp.concatenate(
        [
            mm_lt(jnp.concatenate(n2, axis=0), jnp.concatenate(d_hidden, axis=0)).astype(bf16),
            mm_lt(cot_all, jnp.concatenate(active, axis=0)).astype(bf16),
        ],
        axis=1,
    )
    share2 = lax.psum_scatter(grad2, "dp", scatter_dimension=0, tiled=True).astype(f32)
    d_qkv, input_grad, seq_sums = ([], [], [])
    gain_attn_sum = jnp.zeros((width,), f32)
    for i in seqs:
        d_mixed = mm(d_h1_low[i], w1[:, 3 * shard :]).astype(bf16)
        parts = attend_back(
            query[i],
            key[i],
            value[i],
            same[i],
            scale,
            lse[i],
            d_mixed.reshape(seq_len, heads_dev, head_size),
        )
        d_qkv.append(
            jnp.concatenate([p.reshape(seq_len, shard).astype(bf16) for p in parts], axis=1)
        )
        d_n1 = mm_rt(d_qkv[i], w1[:, : 3 * shard])
        gain_attn_sum = gain_attn_sum + jnp.sum(d_n1 * unit0[i], axis=0)
        term = norm_back(unit0[i], inv0[i], attn_g, d_n1)
        term = jnp.concatenate([term[:half] + d_h1[i] * (1.0 / chips), term[half:]], axis=0)
        seq_sums.append(jnp.sum(term, axis=0))
        input_grad.append(to_features(term.astype(bf16), n_tensor))
    grad1 = jnp.concatenate(
        [
            mm_lt(jnp.concatenate(n1, axis=0), jnp.concatenate(d_qkv, axis=0)).astype(bf16),
            mm_lt(jnp.concatenate(d_h1_low, axis=0), jnp.concatenate(mixed, axis=0)).astype(bf16),
        ],
        axis=1,
    )
    share1 = ring.scatter(grad1)
    sums = jnp.zeros((n_seqs, width), f32)
    sums = lax.dynamic_update_slice_in_dim(sums, jnp.stack(seq_sums), me_dp * seqs_dev, 0)
    sums = jnp.concatenate([sums, gain_attn_sum[None], gain_mlp_sum[None] * (1.0 / chips)], axis=0)
    sums = lax.psum(sums, ("dp", "tensor"))
    rows = width // n_dp
    sums = lax.dynamic_slice_in_dim(sums, me_dp * rows, rows, 1)
    factor = float(n_seqs * seq_len) ** (-0.5)
    grad_time = (
        jnp.einsum("st,sd->td", temb, sums[:n_seqs], precision=lax.Precision.HIGHEST) * factor
    )

    def natural(value):
        return jnp.roll(value, core * half, axis=0)

    share1, share2 = (share1 * factor, share2 * factor)
    return (
        jnp.stack([natural(b) for b in block_out]),
        jnp.stack([natural(g) for g in input_grad]),
        jnp.stack([share1[:, c * shard : (c + 1) * shard] for c in range(3)]),
        share1[:, 3 * shard :].T,
        share2[:, :hidden_dev],
        share2[:, hidden_dev:].T,
        grad_time,
        sums[n_seqs] * factor,
        sums[n_seqs + 1] * factor,
    )


def solution(mesh):
    in_specs = (
        P("dp", None, None),
        P("dp", None),
        P("dp", None),
        P("dp"),
        P(None, "dp", "tensor"),
        P("tensor", "dp"),
        P("dp", "tensor"),
        P("tensor", "dp"),
        P(None, "dp"),
        P("dp"),
        P("dp"),
        P("dp", None, None),
    )
    out_specs = (
        P("dp", None, "tensor"),
        P("dp", None, "tensor"),
        P(None, "dp", "tensor"),
        P("tensor", "dp"),
        P("dp", "tensor"),
        P("tensor", "dp"),
        P(None, "dp"),
        P("dp"),
        P("dp"),
    )
    return jax.shard_map(shards, mesh=mesh, in_specs=in_specs, out_specs=out_specs, check_vma=False)
```

profile of v0, /device:TPU:0, one launch (start us, length us, event | category | flops | bytes accessed | tf_op | source)
XLA Modules:
  0.0 683.9 jit_solution(16655282718602888327)
XLA Ops:
  9.1 3.0 collective-permute-start
  14.9 12.1 %all-reduce = s32[16]{0:T(128)S(1)} all-reduce(s32[16]{0:T(128)S(1)} %dynamic-update-slice), channel_id=1, replica_groups=mesh['dp'=8,'tensor'=4] {'dp'}, use_global_device_ids=true, to_apply=%add | all-reduce | flops 16 | bytes 128
  28.4 31.2 %all_gather.10 = f32[18,1024]{1,0:T(8,128)S(1)} all-gather(f32[18,128]{1,0:T(8,128)S(1)} %pad_maximum_fusion.10), channel_id=1, replica_groups=mesh['dp'=8,'tensor'=4] {'dp'}, dimensions={1}, use_global_device_ids=true | all-gather | bytes 82944 | tf_op jit(solution)/shard_map/all_gather | solution.py:191
  59.7 4.7 slice_bitcast_fusion.3
  64.4 16.2 %multiply_sine_fusion.1 = (f32[1024,512]{1,0:T(8,128)S(1)}, f32[1024,512]{1,0:T(8,128)S(1)}, f32[1024,512]{1,0:T(8,128)}, f32[1024,512]{1,0:T(8,128)}) fusion(f32[512]{0:T(512)S(1)} %multiply_exponential_fusion, f32[1024]{0:T(1024)S(1)} %get-tuple-element.168, f32[1024]{0:T(1024)S(1)} %get-tuple-element.166), kind=kLoop, calls=%fused_computation.119 | loop fusion | flops 1048576 | bytes 8398848 | tf_op jit(solution)/shard_map/sin | solution.py:19
  111.0 4.9 collective-permute-done.6
  118.0 7.5 %fusion.238 = (f32[4,1024]{1,0:T(4,128)S(1)}, f32[4,1024,1024]{1,2,0:T(8,128)}) fusion(bf16[1024,4,64]{0,2,1:T(8,128)(2,1)S(1)} %bitcast.178, bf16[1024,4,64]{0,2,1:T(8,128)(2,1)S(1)} %bitcast.176, pred[1024,1024]{0,1:T(8,128)(4,1)S(1)} %broadcast_compare_fusion.1), kind=kOutput, calls=%fused_computation.439 | convolution fusion | flops 549449728 | bytes 18890752 | tf_op jit(solution)/shard_map/qhe,khe->hqk/dot_general | solution.py:48
  125.5 8.0 %fusion = f32[4,1024]{1,0:T(4,128)S(1)} fusion(f32[4,1024,1024]{1,2,0:T(8,128)} %get-tuple-element.152, f32[4,1024]{1,0:T(4,128)S(1)} %get-tuple-element.151), kind=kLoop, calls=%fused_computation.12 | loop fusion | flops 8384512 | bytes 16809984 | tf_op jit(solution)/shard_map/reduce_sum | solution.py:52
  133.5 7.6 %fusion.144 = bf16[4,64,1024]{2,1,0:T(8,128)(2,1)S(1)} fusion(bf16[1024,4,64]{0,2,1:T(8,128)(2,1)S(1)} %bitcast.188, f32[4,1024,1024]{1,2,0:T(8,128)} %get-tuple-element.152, f32[4,1024]{1,0:T(4,128)S(1)} %fusion, f32[4,1024]{1,0:T(4,128)S(1)} %get-tuple-element.151), kind=kOutput, calls=%fused_computation.250 | convolution fusion | flops 549715968 | bytes 17858560 | tf_op jit(solution)/shard_map/hqk,khe->qhe/dot_general | solution.py:54
  146.3 23.7 %collective-permute-done.8 = bf16[512,1024]{1,0:T(8,128)(2,1)S(1)} collective-permute-done((bf16[512,1024]{1,0:T(8,128)(2,1)S(1)}, bf16[512,1024]{1,0:T(8,128)(2,1)S(1)}, u32[]{:S(2)}, u32[]{:S(2)}) %collective-permute-start.8) | collective-permute-done | bytes 1048608 | tf_op jit(solution)/shard_map/ppermute | solution.py:133
  174.7 4.1 fusion.68
  178.9 4.7 multiply_convert_fusion.4
  183.6 3.7 fusion.17
  194.3 2.9 fusion.225
  203.1 2.9 copy.144
  206.0 12.1 %collective-permute-done.18 = bf16[512,1024]{1,0:T(8,128)(2,1)} collective-permute-done((bf16[512,1024]{1,0:T(8,128)(2,1)S(1)}, bf16[512,1024]{1,0:T(8,128)(2,1)}, u32[]{:S(2)}, u32[]{:S(2)}) %collective-permute-start.18) | collective-permute-done | bytes 1048608 | tf_op jit(solution)/shard_map/ppermute | solution.py:133
  220.8 3.5 fusion.219
  229.7 9.4 %fusion.124 = bf16[4,64,1024]{2,1,0:T(8,128)(2,1)} fusion(bf16[1024,4,64]{0,2,1:T(8,128)(2,1)S(1)} %bitcast.182, f32[4,1024,1024]{1,2,0:T(8,128)} %get-tuple-element.152, f32[4,1024]{1,0:T(4,128)S(1)} %log_add_fusion.1), kind=kOutput, calls=%fused_computation.240 | convolution fusion | flops 545521664 | bytes 17842176 | tf_op jit(solution)/shard_map/hqk,qhe->khe/dot_general | solution.py:63
  239.1 7.6 %multiply_reduce_fusion.1 = (f32[4,1024]{1,0:T(4,128)S(1)}, f32[4,1024,1024]{1,2,0:T(8,128)}) fusion(f32[4,1024,1024]{1,2,0:T(8,128)S(1)} %bitcast.171, f32[4,1024]{1,0:T(4,128)S(1)} %log_add_fusion.1, bf16[1024,4,64]{0,2,1:T(8,128)(2,1)S(1)} %bitcast.183, bf16[1024,4,64]{0,2,1:T(8,128)(2,1)S(1)} %bitcast.189), kind=kOutput, calls=%fused_computation.4 | convolution fusion | flops 549449728 | bytes 34635776 | tf_op jit(solution)/shard_map/qhe,khe->hqk/dot_general | solution.py:62
  246.7 8.3 %multiply_convert_fusion.1 = bf16[4,1024,1024]{1,2,0:T(8,128)(2,1)S(1)} fusion(f32[4,1024,1024]{1,2,0:T(8,128)} %get-tuple-element.156, f32[4,1024,1024]{1,2,0:T(8,128)S(1)} %bitcast.171, f32[4,1024]{1,0:T(4,128)S(1)} %get-tuple-element.155, f32[4,1024]{1,0:T(4,128)S(1)} %log_add_fusion.1), kind=kLoop, calls=%fused_computation.3 | loop fusion | flops 16777216 | bytes 41975808 | tf_op jit(solution)/shard_map/convert_element_type | solution.py:65
  261.0 3.5 multiply_reduce_fusion.3
  264.5 3.5 subtract_multiply_fusion.1
  270.1 7.5 %fusion.239 = (f32[4,1024]{1,0:T(4,128)S(1)}, f32[4,1024,1024]{1,2,0:T(8,128)}) fusion(bf16[1024,4,64]{0,2,1:T(8,128)(2,1)S(1)} %bitcast.174, bf16[1024,4,64]{0,2,1:T(8,128)(2,1)S(1)} %bitcast.172, pred[1024,1024]{0,1:T(8,128)(4,1)S(1)} %broadcast_compare_fusion), kind=kOutput, calls=%fused_computation.440 | convolution fusion | flops 549449728 | bytes 18890752 | tf_op jit(solution)/shard_map/qhe,khe->hqk/dot_general | solution.py:48
  277.5 8.0 %fusion.1 = f32[4,1024]{1,0:T(4,128)S(1)} fusion(f32[4,1024,1024]{1,2,0:T(8,128)} %get-tuple-element.159, f32[4,1024]{1,0:T(4,128)S(1)} %get-tuple-element.158), kind=kLoop, calls=%fused_computation.13 | loop fusion | flops 8384512 | bytes 16809984 | tf_op jit(solution)/shard_map/reduce_sum | solution.py:52
  285.6 7.7 %fusion.143 = bf16[4,64,1024]{2,1,0:T(8,128)(2,1)S(1)} fusion(bf16[1024,4,64]{0,2,1:T(8,128)(2,1)S(1)} %bitcast.186, f32[4,1024,1024]{1,2,0:T(8,128)} %get-tuple-element.159, f32[4,1024]{1,0:T(4,128)S(1)} %fusion.1, f32[4,1024]{1,0:T(4,128)S(1)} %get-tuple-element.158), kind=kOutput, calls=%fused_computation.249 | convolution fusion | flops 549715968 | bytes 17858560 | tf_op jit(solution)/shard_map/hqk,khe->qhe/dot_general | solution.py:54
  298.5 23.7 %collective-permute-done.13 = bf16[512,1024]{1,0:T(8,128)(2,1)S(1)} collective-permute-done((bf16[512,1024]{1,0:T(8,128)(2,1)S(1)}, bf16[512,1024]{1,0:T(8,128)(2,1)S(1)}, u32[]{:S(2)}, u32[]{:S(2)}) %collective-permute-start.13) | collective-permute-done | bytes 1048608 | tf_op jit(solution)/shard_map/ppermute | solution.py:133
  324.3 4.7 fusion.67
  340.2 5.5 multiply_convert_fusion.2
  345.7 3.7 fusion.23
  366.5 3.9 add_convert_fusion
  377.9 2.9 copy.145
  380.8 9.4 %fusion.89 = bf16[1024,1024]{0,1:T(8,128)(2,1)} fusion(bf16[1024,1024]{1,0:T(8,128)(2,1)} %get-tuple-element.160, bf16[1024,1024]{1,0:T(8,128)(2,1)} %copy-done.109, bf16[1024,1024]{1,0:T(8,128)(2,1)} %fusion.67, bf16[1024,1024]{1,0:T(8,128)(2,1)} %fusion.68), kind=kOutput, calls=%fused_computation.203 | convolution fusion | flops 4312793088 | bytes 10485760 | tf_op jit(solution)/shard_map/ki,kj->ij/dot_general | solution.py:80
  390.2 5.9 collective-permute-done.23
  398.6 4.4 fusion.220
  403.2 9.2 %fusion.94 = bf16[1024,1024]{0,1:T(8,128)(2,1)} fusion(bf16[1024,1024]{1,0:T(8,128)(2,1)} %copy-done.108, bf16[1024,1024]{1,0:T(8,128)(2,1)} %copy-done.107, bf16[512,1024]{1,0:T(8,128)(2,1)} %collective-permute-done.14, bf16[512,1024]{1,0:T(8,128)(2,1)} %multiply_convert_fusion.6, bf16[512,1024]{1,0:T(8,128)(2,1)} %collective-permute-done.9, ...), kind=kOutput, calls=%fused_computation.204 | convolution fusion | flops 4321181696 | bytes 10485760 | tf_op jit(solution)/shard_map/ki,kj->ij/dot_general | solution.py:80
  415.5 3.6 fusion.127
  419.0 10.5 %multiply_reduce_fusion = (f32[4,1024]{1,0:T(4,128)S(1)}, f32[4,1024,1024]{1,2,0:T(8,128)}) fusion(f32[4,1024,1024]{1,2,0:T(8,128)S(1)} %bitcast.169, f32[4,1024]{1,0:T(4,128)S(1)} %log_add_fusion, bf16[1024,4,64]{0,2,1:T(8,128)(2,1)} %bitcast.185, bf16[1024,4,64]{0,2,1:T(8,128)(2,1)} %bitcast.187), kind=kOutput, calls=%fused_computation.1 | convolution fusion | flops 549449728 | bytes 34635776 | tf_op jit(solution)/shard_map/qhe,khe->hqk/dot_general | solution.py:62
  429.6 8.0 %multiply_convert_fusion = bf16[4,1024,1024]{1,2,0:T(8,128)(2,1)S(1)} fusion(f32[4,1024,1024]{1,2,0:T(8,128)} %get-tuple-element.163, f32[4,1024,1024]{1,2,0:T(8,128)S(1)} %bitcast.169, f32[4,1024]{1,0:T(4,128)S(1)} %get-tuple-element.162, f32[4,1024]{1,0:T(4,128)S(1)} %log_add_fusion), kind=kLoop, calls=%fused_computation | loop fusion | flops 16777216 | bytes 41975808 | tf_op jit(solution)/shard_map/convert_element_type | solution.py:65
  450.5 4.1 pad_maximum_fusion
  454.6 6.7 copy.139
  483.2 7.7 %collective-permute-done.21 = bf16[1024,1,256]{2,0,1:T(8,128)(2,1)} collective-permute-done((bf16[1024,1,256]{2,0,1:T(8,128)(2,1)}, bf16[1024,1,256]{2,0,1:T(8,128)(2,1)}, u32[]{:S(2)}, u32[]{:S(2)}) %collective-permute-start.21) | collective-permute-done | bytes 524320 | tf_op jit(solution)/shard_map/ppermute | solution.py:133
  499.4 2.9 fusion.140
  503.0 3.4 fusion.99
  520.4 49.7 %all-reduce.3.cloned.1.call-done = f32[18,1024]{1,0:T(8,128)} async-done(((f32[18,1024]{1,0:T(8,128)}), f32[18,1024]{1,0:T(8,128)}) %all-reduce.3.cloned.1.call-update) | async-done | bytes 73744 | tf_op jit(solution)/shard_map/psum | solution.py:312
  573.0 3.3 collective-permute-start.29
  585.8 14.7 %collective-permute-done.32 = bf16[128,1024]{0,1:T(8,128)(2,1)S(1)} collective-permute-done((bf16[128,1024]{0,1:T(8,128)(2,1)S(1)}, bf16[128,1024]{0,1:T(8,128)(2,1)S(1)}, u32[]{:S(2)}, u32[]{:S(2)}) %collective-permute-start.32) | collective-permute-done | bytes 262176 | tf_op jit(solution)/shard_map/ppermute | solution.py:124
  604.5 16.3 %collective-permute-done.33 = bf16[128,1024]{0,1:T(8,128)(2,1)S(1)} collective-permute-done((bf16[128,1024]{0,1:T(8,128)(2,1)S(1)}, bf16[128,1024]{0,1:T(8,128)(2,1)S(1)}, u32[]{:S(2)}, u32[]{:S(2)}) %collective-permute-start.33) | collective-permute-done | bytes 262176 | tf_op jit(solution)/shard_map/ppermute | solution.py:124
  625.9 47.9 %reduce-scatter.4.cloned.1.call-done = bf16[128,2048]{1,0:T(8,128)(2,1)} async-done(((bf16[1024,2048]{1,0:T(8,128)(2,1)}), bf16[128,2048]{1,0:T(8,128)(2,1)}) %reduce-scatter.4.cloned.1.call-update) | async-done | bytes 524304
  (471 shorter events, 193.7 us)
Async XLA Ops:
  7.2 20.7 %copy-start = (bf16[256,128]{1,0:T(8,128)(2,1)S(1)}, bf16[256,128]{1,0:T(8,128)(2,1)}, u32[]{:S(2)}) copy-start(bf16[256,128]{1,0:T(8,128)(2,1)} %param.30) | copy-start | bytes 196612
  7.2 171.6 %all-gather.2.cloned.1.call-start = ((), (), s32[]{:S(2)}) async-start(), calls=%async_computation.1 | async-start | bytes 4718592 | tf_op jit(solution)/shard_map/all_gather | solution.py:184
  8.7 18.3 %copy-start.96 = (s32[2,8]{1,0:T(2,128)S(1)}, s32[2,8]{1,0:T(2,128)}, u32[]{:S(2)}) copy-start(s32[2,8]{1,0:T(2,128)} %param.24) | copy-start | bytes 196
  8.7 18.3 %copy-start.94 = (s32[2,1024]{1,0:T(2,128)S(1)}, s32[2,1024]{1,0:T(2,128)}, u32[]{:S(2)}) copy-start(s32[2,1024]{1,0:T(2,128)} %param.23) | copy-start | bytes 24580
  8.7 19.0 %copy-start.97 = (bf16[128]{0:T(256)(128)(2,1)S(1)}, bf16[128]{0:T(256)(128)(2,1)}, u32[]{:S(2)}) copy-start(bf16[128]{0:T(256)(128)(2,1)} %param.32) | copy-start | bytes 772
  8.7 19.0 %copy-start.98 = (bf16[128]{0:T(256)(128)(2,1)S(1)}, bf16[128]{0:T(256)(128)(2,1)}, u32[]{:S(2)}) copy-start(bf16[128]{0:T(256)(128)(2,1)} %param.31) | copy-start | bytes 772
  9.1 77.5 %collective-permute-start = (bf16[128,1024]{0,1:T(8,128)(2,1)S(1)}, bf16[128,1024]{0,1:T(8,128)(2,1)}, u32[]{:S(2)}, u32[]{:S(2)}) collective-permute-start(bf16[128,1024]{0,1:T(8,128)(2,1)S(1)} %get-tuple-element.117), channel_id=1, source_target_pairs={{8,0},{16,8},{24,16},{28,24},{20,28},{12,20},{4,12},{0,4},{9,1},{1... | collective-permute-start | bytes 786440 | tf_op jit(solution)/shard_map/ppermute | solution.py:106
  12.1 74.6 %collective-permute-start.1 = (bf16[128,1024]{0,1:T(8,128)(2,1)S(1)}, bf16[128,1024]{0,1:T(8,128)(2,1)S(1)}, u32[]{:S(2)}, u32[]{:S(2)}) collective-permute-start(bf16[128,1024]{0,1:T(8,128)(2,1)S(1)} %get-tuple-element.117), channel_id=1, source_target_pairs={{0,8},{8,16},{16,24},{24,28},{28,20},{20,12},{12,4},{4,0},{1,9},{9... | collective-permute-start | bytes 786440 | tf_op jit(solution)/shard_map/ppermute | solution.py:104
  13.3 556.8 %all-reduce.3.cloned.1.call-start = ((), (), s32[]{:S(2)}) async-start(), calls=%async_computation.2 | async-start | bytes 196608 | tf_op jit(solution)/shard_map/psum | solution.py:312
  86.6 17.2 %collective-permute-start.2 = (bf16[128,1024]{0,1:T(8,128)(2,1)}, bf16[128,1024]{0,1:T(8,128)(2,1)}, u32[]{:S(2)}, u32[]{:S(2)}) collective-permute-start(bf16[128,1024]{0,1:T(8,128)(2,1)} %collective-permute-done), channel_id=1, source_target_pairs={{8,0},{16,8},{24,16},{28,24},{20,28},{12,20},{4,12},{0,4},{9,1},{1... | collective-permute-start | bytes 786440 | tf_op jit(solution)/shard_map/ppermute | solution.py:106
  86.6 15.7 %collective-permute-start.3 = (bf16[128,1024]{0,1:T(8,128)(2,1)S(1)}, bf16[128,1024]{0,1:T(8,128)(2,1)}, u32[]{:S(2)}, u32[]{:S(2)}) collective-permute-start(bf16[128,1024]{0,1:T(8,128)(2,1)S(1)} %collective-permute-done.1), channel_id=1, source_target_pairs={{0,8},{8,16},{16,24},{24,28},{28,20},{20,12},{12,4},{4,0},{1,9},{9... | collective-permute-start | bytes 786440 | tf_op jit(solution)/shard_map/ppermute | solution.py:104
  102.4 6.6 collective-permute-start.5
  103.8 6.9 %collective-permute-start.4 = (bf16[128,1024]{0,1:T(8,128)(2,1)}, bf16[128,1024]{0,1:T(8,128)(2,1)S(1)}, u32[]{:S(2)}, u32[]{:S(2)}) collective-permute-start(bf16[128,1024]{0,1:T(8,128)(2,1)} %collective-permute-done.2), channel_id=1, source_target_pairs={{8,0},{16,8},{24,16},{28,24},{20,28},{12,20},{4,12},{0,4},{9,1},{1... | collective-permute-start | bytes 786440 | tf_op jit(solution)/shard_map/ppermute | solution.py:106
  109.0 6.9 %collective-permute-start.6 = (bf16[128,1024]{0,1:T(8,128)(2,1)S(1)}, bf16[128,1024]{0,1:T(8,128)(2,1)S(1)}, u32[]{:S(2)}, u32[]{:S(2)}) collective-permute-start(bf16[128,1024]{0,1:T(8,128)(2,1)S(1)} %collective-permute-done.5), channel_id=1, source_target_pairs={{0,8},{8,16},{16,24},{24,28},{28,20},{20,12},{12,4},{4,0},{1,9},{9... | collective-permute-start | bytes 786440 | tf_op jit(solution)/shard_map/ppermute | solution.py:104
  116.0 25.7 %copy-start.14 = (bf16[1024,1024]{0,1:T(8,128)(2,1)}, bf16[1024,1024]{0,1:T(8,128)(2,1)S(1)}, u32[]{:S(2)}) copy-start(bf16[1024,1024]{0,1:T(8,128)(2,1)S(1)} %constant_dynamic-update-slice_fusion.1) | copy-start | bytes 6291460
  141.6 2.7 collective-permute-start.7
  141.7 28.3 %copy-start.6 = (f32[1024,1024]{1,0:T(8,128)S(1)}, f32[1024,1024]{1,0:T(8,128)}, u32[]{:S(2)}) copy-start(f32[1024,1024]{1,0:T(8,128)} %copy-done.5) | copy-start | bytes 12582916
  144.7 25.3 %collective-permute-start.8 = (bf16[512,1024]{1,0:T(8,128)(2,1)S(1)}, bf16[512,1024]{1,0:T(8,128)(2,1)S(1)}, u32[]{:S(2)}, u32[]{:S(2)}) collective-permute-start(bf16[512,1024]{1,0:T(8,128)(2,1)S(1)} %add_convert_fusion.5), channel_id=1, source_target_pairs={{0,2},{1,3},{2,0},{3,1},{4,6},{5,7},{6,4},{7,5},{8,10},{9,11},{10,... | collective-permute-start | bytes 3145736 | tf_op jit(solution)/shard_map/ppermute | solution.py:133
  171.1 7.7 %collective-permute-start.9 = (bf16[512,1024]{1,0:T(8,128)(2,1)S(1)}, bf16[512,1024]{1,0:T(8,128)(2,1)}, u32[]{:S(2)}, u32[]{:S(2)}) collective-permute-start(bf16[512,1024]{1,0:T(8,128)(2,1)S(1)} %multiply_convert_fusion.7), channel_id=1, source_target_pairs={{0,1},{1,0},{2,3},{3,2},{4,5},{5,4},{6,7},{7,6},{8,9},{9,8},{10,11... | collective-permute-start | bytes 3145736 | tf_op jit(solution)/shard_map/ppermute | solution.py:133
  188.7 2.7 collective-permute-start.17
  192.7 25.4 %collective-permute-start.18 = (bf16[512,1024]{1,0:T(8,128)(2,1)S(1)}, bf16[512,1024]{1,0:T(8,128)(2,1)}, u32[]{:S(2)}, u32[]{:S(2)}) collective-permute-start(bf16[512,1024]{1,0:T(8,128)(2,1)S(1)} %add_convert_fusion.1), channel_id=1, source_target_pairs={{0,2},{1,3},{2,0},{3,1},{4,6},{5,7},{6,4},{7,5},{8,10},{9,11},{10,... | collective-permute-start | bytes 3145736 | tf_op jit(solution)/shard_map/ppermute | solution.py:133
  220.8 18.3 %slice-start.4 = ((s8[16777216]{0:T(1024)(128)(4,1)}), s8[4194304]{0:T(1024)(128)(4,1)S(1)}, s32[]{:S(2)}) async-start(s8[16777216]{0:T(1024)(128)(4,1)} %bitcast.170), calls=%async_computation.8 | async-start | bytes 8388608
  224.4 2.7 collective-permute-start.19
  293.8 2.7 collective-permute-start.12
  296.9 25.3 %collective-permute-start.13 = (bf16[512,1024]{1,0:T(8,128)(2,1)S(1)}, bf16[512,1024]{1,0:T(8,128)(2,1)S(1)}, u32[]{:S(2)}, u32[]{:S(2)}) collective-permute-start(bf16[512,1024]{1,0:T(8,128)(2,1)S(1)} %add_convert_fusion.3), channel_id=1, source_target_pairs={{0,2},{1,3},{2,0},{3,1},{4,6},{5,7},{6,4},{7,5},{8,10},{9,11},{10,... | collective-permute-start | bytes 3145736 | tf_op jit(solution)/shard_map/ppermute | solution.py:133
  324.3 15.6 %collective-permute-start.14 = (bf16[512,1024]{1,0:T(8,128)(2,1)}, bf16[512,1024]{1,0:T(8,128)(2,1)}, u32[]{:S(2)}, u32[]{:S(2)}) collective-permute-start(bf16[512,1024]{1,0:T(8,128)(2,1)} %multiply_convert_fusion.6), channel_id=1, source_target_pairs={{0,1},{1,0},{2,3},{3,2},{4,5},{5,4},{6,7},{7,6},{8,9},{9,8},{10,11... | collective-permute-start | bytes 3145736 | tf_op jit(solution)/shard_map/ppermute | solution.py:133
  339.5 121.9 %collective-permute-start.10 = (bf16[1024,2,256]{2,0,1:T(8,128)(2,1)}, bf16[1024,2,256]{2,0,1:T(8,128)(2,1)}, u32[]{:S(2)}, u32[]{:S(2)}) collective-permute-start(bf16[1024,2,256]{2,0,1:T(8,128)(2,1)} %fusion.154), channel_id=1, source_target_pairs={{0,1},{1,0},{2,3},{3,2},{4,5},{5,4},{6,7},{7,6},{8,9},{9,8},{10,11... | collective-permute-start | bytes 3145736 | tf_op jit(solution)/shard_map/ppermute | solution.py:133
  351.7 14.5 %collective-permute-start.22 = (bf16[512,1024]{1,0:T(8,128)(2,1)}, bf16[512,1024]{1,0:T(8,128)(2,1)}, u32[]{:S(2)}, u32[]{:S(2)}) collective-permute-start(bf16[512,1024]{1,0:T(8,128)(2,1)} %convolution_convert_fusion.2), channel_id=1, source_target_pairs={{0,1},{1,0},{2,3},{3,2},{4,5},{5,4},{6,7},{7,6},{8,9},{9,8},{10,11... | collective-permute-start | bytes 3145736 | tf_op jit(solution)/shard_map/ppermute | solution.py:133
  365.6 100.3 %collective-permute-start.20 = (bf16[1024,2,256]{2,0,1:T(8,128)(2,1)}, bf16[1024,2,256]{2,0,1:T(8,128)(2,1)}, u32[]{:S(2)}, u32[]{:S(2)}) collective-permute-start(bf16[1024,2,256]{2,0,1:T(8,128)(2,1)} %dynamic-slice_bitcast_fusion.1), channel_id=1, source_target_pairs={{0,1},{1,0},{2,3},{3,2},{4,5},{5,4},{6,7},{7,6},{8,9},{9,8},{10,11... | collective-permute-start | bytes 3145736 | tf_op jit(solution)/shard_map/ppermute | solution.py:133
  370.4 25.7 %collective-permute-start.23 = (bf16[512,1024]{1,0:T(8,128)(2,1)}, bf16[512,1024]{1,0:T(8,128)(2,1)}, u32[]{:S(2)}, u32[]{:S(2)}) collective-permute-start(bf16[512,1024]{1,0:T(8,128)(2,1)} %add_convert_fusion), channel_id=1, source_target_pairs={{0,2},{1,3},{2,0},{3,1},{4,6},{5,7},{6,4},{7,5},{8,10},{9,11},{10,... | collective-permute-start | bytes 3145736 | tf_op jit(solution)/shard_map/ppermute | solution.py:133
  403.1 9.3 %collective-permute-start.24 = (bf16[512,1024]{1,0:T(8,128)(2,1)}, bf16[512,1024]{1,0:T(8,128)(2,1)}, u32[]{:S(2)}, u32[]{:S(2)}) collective-permute-start(bf16[512,1024]{1,0:T(8,128)(2,1)} %get-tuple-element.71), channel_id=1, source_target_pairs={{0,1},{1,0},{2,3},{3,2},{4,5},{5,4},{6,7},{7,6},{8,9},{9,8},{10,11... | collective-permute-start | bytes 3145736 | tf_op jit(solution)/shard_map/ppermute | solution.py:133
  450.2 223.6 %reduce-scatter.4.cloned.1.call-start = ((), (), s32[]{:S(2)}) async-start(), calls=%async_computation.3 | async-start | bytes 4718592
  464.4 15.1 %collective-permute-start.11 = (bf16[1024,1,256]{2,0,1:T(8,128)(2,1)}, bf16[1024,1,256]{2,0,1:T(8,128)(2,1)}, u32[]{:S(2)}, u32[]{:S(2)}) collective-permute-start(bf16[1024,1,256]{2,0,1:T(8,128)(2,1)} %dynamic-slice_convert_fusion.3), channel_id=1, source_target_pairs={{0,2},{1,3},{2,0},{3,1},{4,6},{5,7},{6,4},{7,5},{8,10},{9,11},{10,... | collective-permute-start | bytes 1572872 | tf_op jit(solution)/shard_map/ppermute | solution.py:133
  473.2 23.1 %collective-permute-start.15 = (bf16[1024,2,256]{2,0,1:T(8,128)(2,1)}, bf16[1024,2,256]{2,0,1:T(8,128)(2,1)S(1)}, u32[]{:S(2)}, u32[]{:S(2)}) collective-permute-start(bf16[1024,2,256]{2,0,1:T(8,128)(2,1)} %fusion.150), channel_id=1, source_target_pairs={{0,1},{1,0},{2,3},{3,2},{4,5},{5,4},{6,7},{7,6},{8,9},{9,8},{10,11... | collective-permute-start | bytes 3145736 | tf_op jit(solution)/shard_map/ppermute | solution.py:133
  476.0 15.0 %collective-permute-start.21 = (bf16[1024,1,256]{2,0,1:T(8,128)(2,1)}, bf16[1024,1,256]{2,0,1:T(8,128)(2,1)}, u32[]{:S(2)}, u32[]{:S(2)}) collective-permute-start(bf16[1024,1,256]{2,0,1:T(8,128)(2,1)} %dynamic-slice_convert_fusion.1), channel_id=1, source_target_pairs={{0,2},{1,3},{2,0},{3,1},{4,6},{5,7},{6,4},{7,5},{8,10},{9,11},{10,... | collective-permute-start | bytes 1572872 | tf_op jit(solution)/shard_map/ppermute | solution.py:133
  497.7 80.0 %collective-permute-start.16 = (bf16[1024,1,256]{2,0,1:T(8,128)(2,1)}, bf16[1024,1,256]{2,0,1:T(8,128)(2,1)}, u32[]{:S(2)}, u32[]{:S(2)}) collective-permute-start(bf16[1024,1,256]{2,0,1:T(8,128)(2,1)} %dynamic-slice_convert_fusion.2), channel_id=1, source_target_pairs={{0,2},{1,3},{2,0},{3,1},{4,6},{5,7},{6,4},{7,5},{8,10},{9,11},{10,... | collective-permute-start | bytes 1572872 | tf_op jit(solution)/shard_map/ppermute | solution.py:133
  507.4 8.2 %collective-permute-start.27 = (bf16[128,1024]{0,1:T(8,128)(2,1)}, bf16[128,1024]{0,1:T(8,128)(2,1)}, u32[]{:S(2)}, u32[]{:S(2)}) collective-permute-start(bf16[128,1024]{0,1:T(8,128)(2,1)} %get-tuple-element.89), channel_id=1, source_target_pairs={{0,8},{8,16},{16,24},{24,28},{28,20},{20,12},{12,4},{4,0},{1,9},{9... | collective-permute-start | bytes 786440 | tf_op jit(solution)/shard_map/ppermute | solution.py:124
  507.7 71.2 %collective-permute-start.31 = (bf16[128,1024]{0,1:T(8,128)(2,1)}, bf16[128,1024]{0,1:T(8,128)(2,1)S(1)}, u32[]{:S(2)}, u32[]{:S(2)}) collective-permute-start(bf16[128,1024]{0,1:T(8,128)(2,1)} %get-tuple-element.90), channel_id=1, source_target_pairs={{8,0},{16,8},{24,16},{28,24},{20,28},{12,20},{4,12},{0,4},{9,1},{1... | collective-permute-start | bytes 786440 | tf_op jit(solution)/shard_map/ppermute | solution.py:124
  517.4 52.7 %copy-start.88 = (f32[16,128]{1,0:T(8,128)S(1)}, f32[16,128]{1,0:T(8,128)}, u32[]{:S(2)}) copy-start(f32[16,128]{1,0:T(8,128)} %copy-done.87) | copy-start | bytes 24580
  517.4 52.7 %copy-start.90 = (f32[16,128]{1,0:T(8,128)S(1)}, f32[16,128]{1,0:T(8,128)}, u32[]{:S(2)}) copy-start(f32[16,128]{1,0:T(8,128)} %copy-done.89) | copy-start | bytes 24580
  517.4 54.6 %collective-permute-start.28 = (bf16[128,1024]{0,1:T(8,128)(2,1)}, bf16[128,1024]{0,1:T(8,128)(2,1)}, u32[]{:S(2)}, u32[]{:S(2)}) collective-permute-start(bf16[128,1024]{0,1:T(8,128)(2,1)} %add_convert_fusion.12), channel_id=1, source_target_pairs={{0,8},{8,16},{16,24},{24,28},{28,20},{20,12},{12,4},{4,0},{1,9},{9... | collective-permute-start | bytes 786440 | tf_op jit(solution)/shard_map/ppermute | solution.py:124
  520.4 80.2 %collective-permute-start.25 = (bf16[1024,2,256]{2,0,1:T(8,128)(2,1)}, bf16[1024,2,256]{2,0,1:T(8,128)(2,1)S(1)}, u32[]{:S(2)}, u32[]{:S(2)}) collective-permute-start(bf16[1024,2,256]{2,0,1:T(8,128)(2,1)} %dynamic-slice_bitcast_fusion), channel_id=1, source_target_pairs={{0,1},{1,0},{2,3},{3,2},{4,5},{5,4},{6,7},{7,6},{8,9},{9,8},{10,11... | collective-permute-start | bytes 3145736 | tf_op jit(solution)/shard_map/ppermute | solution.py:133
  573.0 7.8 %collective-permute-start.29 = (bf16[128,1024]{0,1:T(8,128)(2,1)S(1)}, bf16[128,1024]{0,1:T(8,128)(2,1)S(1)}, u32[]{:S(2)}, u32[]{:S(2)}) collective-permute-start(bf16[128,1024]{0,1:T(8,128)(2,1)S(1)} %add_convert_fusion.11), channel_id=1, source_target_pairs={{0,8},{8,16},{16,24},{24,28},{28,20},{20,12},{12,4},{4,0},{1,9},{9... | collective-permute-start | bytes 786440 | tf_op jit(solution)/shard_map/ppermute | solution.py:124
  581.0 19.4 %collective-permute-start.32 = (bf16[128,1024]{0,1:T(8,128)(2,1)S(1)}, bf16[128,1024]{0,1:T(8,128)(2,1)S(1)}, u32[]{:S(2)}, u32[]{:S(2)}) collective-permute-start(bf16[128,1024]{0,1:T(8,128)(2,1)S(1)} %get-tuple-element.88), channel_id=1, source_target_pairs={{8,0},{16,8},{24,16},{28,24},{20,28},{12,20},{4,12},{0,4},{9,1},{1... | collective-permute-start | bytes 786440 | tf_op jit(solution)/shard_map/ppermute | solution.py:124
  585.2 19.2 %collective-permute-start.30 = (bf16[128,1024]{0,1:T(8,128)(2,1)S(1)}, bf16[128,1024]{0,1:T(8,128)(2,1)S(1)}, u32[]{:S(2)}, u32[]{:S(2)}) collective-permute-start(bf16[128,1024]{0,1:T(8,128)(2,1)S(1)} %get-tuple-element.87), channel_id=1, source_target_pairs={{0,8},{8,16},{16,24},{24,28},{28,20},{20,12},{12,4},{4,0},{1,9},{9... | collective-permute-start | bytes 786440 | tf_op jit(solution)/shard_map/ppermute | solution.py:124
  600.5 20.2 %collective-permute-start.33 = (bf16[128,1024]{0,1:T(8,128)(2,1)S(1)}, bf16[128,1024]{0,1:T(8,128)(2,1)S(1)}, u32[]{:S(2)}, u32[]{:S(2)}) collective-permute-start(bf16[128,1024]{0,1:T(8,128)(2,1)S(1)} %add_convert_fusion.8), channel_id=1, source_target_pairs={{8,0},{16,8},{24,16},{28,24},{20,28},{12,20},{4,12},{0,4},{9,1},{1... | collective-permute-start | bytes 786440 | tf_op jit(solution)/shard_map/ppermute | solution.py:124
  602.4 18.5 %copy-start.30 = (f32[1024,2,256]{2,0,1:T(8,128)}, f32[1024,2,256]{2,0,1:T(8,128)S(1)}, u32[]{:S(2)}) copy-start(f32[1024,2,256]{2,0,1:T(8,128)S(1)} %maximum_add_fusion.5) | copy-start | bytes 6291460
  602.5 20.1 %collective-permute-start.26 = (bf16[1024,1,256]{2,0,1:T(8,128)(2,1)S(1)}, bf16[1024,1,256]{2,0,1:T(8,128)(2,1)S(1)}, u32[]{:S(2)}, u32[]{:S(2)}) collective-permute-start(bf16[1024,1,256]{2,0,1:T(8,128)(2,1)S(1)} %dynamic-slice_convert_fusion), channel_id=1, source_target_pairs={{0,2},{1,3},{2,0},{3,1},{4,6},{5,7},{6,4},{7,5},{8,10},{9,11},{10,... | collective-permute-start | bytes 1572872 | tf_op jit(solution)/shard_map/ppermute | solution.py:133
  (108 other events, 575.6 us)
Sparse Core Ops, SparseCore 0:
  13.4 80.6 all-gather.1
  450.4 119.6 all-reduce.2
  573.7 100.0 reduce-scatter.3
where the time goes:
time: 692 us; the launch traced here: 684 us
  waiting for transfers between devices  223 us (32%)
  matrix products  145 us (21%)
  other arithmetic  122 us (18%)
  local copies, waits for them, and re-layouts  90.8 us (13%)
  blocking collectives  43.3 us (6%)
  starting transfers between devices  30.4 us (4%)
  between operations  29.9 us (4%)
    ppermute x20, waiting for transfers between devices, swap(): return lax.ppermute(value, 'tensor', [(i, i ^ bit) for i in range(n)])  82.7 us
    psum x1, waiting for transfers between devices, shards(): sums = lax.psum(sums, ('dp', 'tensor'))  49.7 us
    unnamed x4, waiting for transfers between devices  47.9 us
    unnamed x253, local copies, waits for them, and re-layouts  38.4 us
    ppermute x7, waiting for transfers between devices, scatter(): run = lax.ppermute(run.astype(bf16), 'dp', way).astype(f32)  35.6 us
    all_gather x1, blocking collectives, shards(): small = lax.all_gather(small, 'dp', axis=1, tiled=True)  31.2 us
    dot_general x8, matrix products, mm(): return jnp.dot(left, right, preferred_element_type=f32)  26.2 us
    dot_general x4, matrix products, mm_lt(): return jnp.einsum('ki,kj->ij', left, right, preferred_element_type=f32)  25 us
  transfers between devices with their start and end apart: 37, of which 18 were waited for; matrix products, arithmetic and copies ran while one was open for 36% of the time, Pallas kernels for 0%

commit v1 on v0

--- a/solution.py
+++ b/solution.py
@@ -309,7 +309,8 @@
     sums = jnp.zeros((n_seqs, width), f32)
     sums = lax.dynamic_update_slice_in_dim(sums, jnp.stack(seq_sums), me_dp * seqs_dev, 0)
     sums = jnp.concatenate([sums, gain_attn_sum[None], gain_mlp_sum[None] * (1.0 / chips)], axis=0)
-    sums = lax.psum(sums, ("dp", "tensor"))
+    bring_stocks = lambda patch, mesh_ax, mesh_dim: lax.psum(lax.psum(patch, mesh_ax), mesh_dim)
+    sums = bring_stocks(sums, "tensor", "dp")
     rows = width // n_dp
     sums = lax.dynamic_slice_in_dim(sums, me_dp * rows, rows, 1)
     factor = float(n_seqs * seq_len) ** (-0.5)

time: 692 us -> 665 us (0.961)
  waiting for transfers between devices: 223 us -> 202 us
    psum x1 -> x2, waiting for transfers between devices: 49.7 us -> 24.7 us  [the longest x1 20.9 us: shards(): lax.psum(patch, mesh_ax)]
    unnamed x4 -> x5, waiting for transfers between devices: 47.9 us -> 51.2 us
    unnamed x253 -> x259, local copies, waits for them, and re-layouts: 38.4 us -> 38.4 us
  transfers between devices with their start and end apart: 37 -> 38, of which waited for: 18 -> 18; matrix products, arithmetic and copies ran while one was open for 36% -> 36% of each run, Pallas kernels for 0% -> 0%
where the time goes in v1:
time: 665 us; the launch traced here: 657 us
  waiting for transfers between devices  202 us (30%)
  matrix products  141 us (21%)
  other arithmetic  121 us (18%)
  local copies, waits for them, and re-layouts  92.3 us (14%)
  blocking collectives  43.3 us (7%)
  between operations  30.3 us (5%)
  starting transfers between devices  27.1 us (4%)
    ppermute x20, waiting for transfers between devices, swap(): return lax.ppermute(value, 'tensor', [(i, i ^ bit) for i in range(n)])  88.2 us
    unnamed x5, waiting for transfers between devices  51.2 us
    unnamed x259, local copies, waits for them, and re-layouts  38.4 us
    all_gather x1, blocking collectives, shards(): small = lax.all_gather(small, 'dp', axis=1, tiled=True)  31.2 us
    ppermute x7, waiting for transfers between devices, scatter(): run = lax.ppermute(run.astype(bf16), 'dp', way).astype(f32)  30.7 us
    dot_general x8, matrix products, mm(): return jnp.dot(left, right, preferred_element_type=f32)  24.2 us
    dot_general x4, matrix products, mm_lt(): return jnp.einsum('ki,kj->ij', left, right, preferred_element_type=f32)  23.8 us
    dot_general x12, matrix products, mm_rt(): return jnp.einsum('ik,jk->ij', left, right, preferred_element_type=f32)  21.6 us
  transfers between devices with their start and end apart: 38, of which 18 were waited for; matrix products, arithmetic and copies ran while one was open for 36% of the time, Pallas kernels for 0%

profile of v1, /device:TPU:0, one launch (start us, length us, event | category | flops | bytes accessed | tf_op | source)
XLA Modules:
  0.0 657.2 jit_solution(4835459991298632572)
XLA Ops:
  9.1 3.0 collective-permute-start
  14.9 12.1 %all-reduce = s32[16]{0:T(128)S(1)} all-reduce(s32[16]{0:T(128)S(1)} %dynamic-update-slice), channel_id=1, replica_groups=mesh['dp'=8,'tensor'=4] {'dp'}, use_global_device_ids=true, to_apply=%add | all-reduce | flops 16 | bytes 128
  28.4 31.2 %all_gather.10 = f32[18,1024]{1,0:T(8,128)S(1)} all-gather(f32[18,128]{1,0:T(8,128)S(1)} %pad_maximum_fusion.10), channel_id=1, replica_groups=mesh['dp'=8,'tensor'=4] {'dp'}, dimensions={1}, use_global_device_ids=true | all-gather | bytes 82944 | tf_op jit(solution)/shard_map/all_gather | solution.py:191
  59.7 4.7 slice_bitcast_fusion.3
  64.4 16.2 %multiply_sine_fusion.1 = (f32[1024,512]{1,0:T(8,128)S(1)}, f32[1024,512]{1,0:T(8,128)S(1)}, f32[1024,512]{1,0:T(8,128)}, f32[1024,512]{1,0:T(8,128)}) fusion(f32[512]{0:T(512)S(1)} %multiply_exponential_fusion, f32[1024]{0:T(1024)S(1)} %get-tuple-element.168, f32[1024]{0:T(1024)S(1)} %get-tuple-element.166), kind=kLoop, calls=%fused_computation.119 | loop fusion | flops 1048576 | bytes 8398848 | tf_op jit(solution)/shard_map/sin | solution.py:19
  111.0 4.9 collective-permute-done.6
  118.1 7.4 %fusion.238 = (f32[4,1024]{1,0:T(4,128)S(1)}, f32[4,1024,1024]{1,2,0:T(8,128)}) fusion(bf16[1024,4,64]{0,2,1:T(8,128)(2,1)S(1)} %bitcast.178, bf16[1024,4,64]{0,2,1:T(8,128)(2,1)S(1)} %bitcast.176, pred[1024,1024]{0,1:T(8,128)(4,1)S(1)} %broadcast_compare_fusion.1), kind=kOutput, calls=%fused_computation.439 | convolution fusion | flops 549449728 | bytes 18890752 | tf_op jit(solution)/shard_map/qhe,khe->hqk/dot_general | solution.py:48
  125.5 8.0 %fusion = f32[4,1024]{1,0:T(4,128)S(1)} fusion(f32[4,1024,1024]{1,2,0:T(8,128)} %get-tuple-element.152, f32[4,1024]{1,0:T(4,128)S(1)} %get-tuple-element.151), kind=kLoop, calls=%fused_computation.12 | loop fusion | flops 8384512 | bytes 16809984 | tf_op jit(solution)/shard_map/reduce_sum | solution.py:52
  133.5 7.6 %fusion.144 = bf16[4,64,1024]{2,1,0:T(8,128)(2,1)S(1)} fusion(bf16[1024,4,64]{0,2,1:T(8,128)(2,1)S(1)} %bitcast.188, f32[4,1024,1024]{1,2,0:T(8,128)} %get-tuple-element.152, f32[4,1024]{1,0:T(4,128)S(1)} %fusion, f32[4,1024]{1,0:T(4,128)S(1)} %get-tuple-element.151), kind=kOutput, calls=%fused_computation.250 | convolution fusion | flops 549715968 | bytes 17858560 | tf_op jit(solution)/shard_map/hqk,khe->qhe/dot_general | solution.py:54
  146.3 23.7 %collective-permute-done.8 = bf16[512,1024]{1,0:T(8,128)(2,1)S(1)} collective-permute-done((bf16[512,1024]{1,0:T(8,128)(2,1)S(1)}, bf16[512,1024]{1,0:T(8,128)(2,1)S(1)}, u32[]{:S(2)}, u32[]{:S(2)}) %collective-permute-start.8) | collective-permute-done | bytes 1048608 | tf_op jit(solution)/shard_map/ppermute | solution.py:133
  174.8 4.2 fusion.68
  179.0 4.7 multiply_convert_fusion.4
  183.8 3.7 fusion.17
  194.4 2.9 fusion.225
  203.2 2.9 copy.144
  206.1 12.0 %collective-permute-done.18 = bf16[512,1024]{1,0:T(8,128)(2,1)} collective-permute-done((bf16[512,1024]{1,0:T(8,128)(2,1)S(1)}, bf16[512,1024]{1,0:T(8,128)(2,1)}, u32[]{:S(2)}, u32[]{:S(2)}) %collective-permute-start.18) | collective-permute-done | bytes 1048608 | tf_op jit(solution)/shard_map/ppermute | solution.py:133
  220.4 3.5 fusion.219
  229.2 9.4 %fusion.124 = bf16[4,64,1024]{2,1,0:T(8,128)(2,1)} fusion(bf16[1024,4,64]{0,2,1:T(8,128)(2,1)S(1)} %bitcast.182, f32[4,1024,1024]{1,2,0:T(8,128)} %get-tuple-element.152, f32[4,1024]{1,0:T(4,128)S(1)} %log_add_fusion.1), kind=kOutput, calls=%fused_computation.240 | convolution fusion | flops 545521664 | bytes 17842176 | tf_op jit(solution)/shard_map/hqk,qhe->khe/dot_general | solution.py:63
  238.6 7.6 %multiply_reduce_fusion.1 = (f32[4,1024]{1,0:T(4,128)S(1)}, f32[4,1024,1024]{1,2,0:T(8,128)}) fusion(f32[4,1024,1024]{1,2,0:T(8,128)S(1)} %bitcast.171, f32[4,1024]{1,0:T(4,128)S(1)} %log_add_fusion.1, bf16[1024,4,64]{0,2,1:T(8,128)(2,1)S(1)} %bitcast.183, bf16[1024,4,64]{0,2,1:T(8,128)(2,1)S(1)} %bitcast.189), kind=kOutput, calls=%fused_computation.4 | convolution fusion | flops 549449728 | bytes 34635776 | tf_op jit(solution)/shard_map/qhe,khe->hqk/dot_general | solution.py:62
  246.2 8.3 %multiply_convert_fusion.1 = bf16[4,1024,1024]{1,2,0:T(8,128)(2,1)S(1)} fusion(f32[4,1024,1024]{1,2,0:T(8,128)} %get-tuple-element.156, f32[4,1024,1024]{1,2,0:T(8,128)S(1)} %bitcast.171, f32[4,1024]{1,0:T(4,128)S(1)} %get-tuple-element.155, f32[4,1024]{1,0:T(4,128)S(1)} %log_add_fusion.1), kind=kLoop, calls=%fused_computation.3 | loop fusion | flops 16777216 | bytes 41975808 | tf_op jit(solution)/shard_map/convert_element_type | solution.py:65
  260.5 3.0 multiply_reduce_fusion.3
  263.6 3.5 subtract_multiply_fusion.1
  269.1 7.4 %fusion.239 = (f32[4,1024]{1,0:T(4,128)S(1)}, f32[4,1024,1024]{1,2,0:T(8,128)}) fusion(bf16[1024,4,64]{0,2,1:T(8,128)(2,1)S(1)} %bitcast.174, bf16[1024,4,64]{0,2,1:T(8,128)(2,1)S(1)} %bitcast.172, pred[1024,1024]{0,1:T(8,128)(4,1)S(1)} %broadcast_compare_fusion), kind=kOutput, calls=%fused_computation.440 | convolution fusion | flops 549449728 | bytes 18890752 | tf_op jit(solution)/shard_map/qhe,khe->hqk/dot_general | solution.py:48
  276.5 8.0 %fusion.1 = f32[4,1024]{1,0:T(4,128)S(1)} fusion(f32[4,1024,1024]{1,2,0:T(8,128)} %get-tuple-element.159, f32[4,1024]{1,0:T(4,128)S(1)} %get-tuple-element.158), kind=kLoop, calls=%fused_computation.13 | loop fusion | flops 8384512 | bytes 16809984 | tf_op jit(solution)/shard_map/reduce_sum | solution.py:52
  284.6 7.7 %fusion.143 = bf16[4,64,1024]{2,1,0:T(8,128)(2,1)S(1)} fusion(bf16[1024,4,64]{0,2,1:T(8,128)(2,1)S(1)} %bitcast.186, f32[4,1024,1024]{1,2,0:T(8,128)} %get-tuple-element.159, f32[4,1024]{1,0:T(4,128)S(1)} %fusion.1, f32[4,1024]{1,0:T(4,128)S(1)} %get-tuple-element.158), kind=kOutput, calls=%fused_computation.249 | convolution fusion | flops 549715968 | bytes 17858560 | tf_op jit(solution)/shard_map/hqk,khe->qhe/dot_general | solution.py:54
  297.5 23.7 %collective-permute-done.13 = bf16[512,1024]{1,0:T(8,128)(2,1)S(1)} collective-permute-done((bf16[512,1024]{1,0:T(8,128)(2,1)S(1)}, bf16[512,1024]{1,0:T(8,128)(2,1)S(1)}, u32[]{:S(2)}, u32[]{:S(2)}) %collective-permute-start.13) | collective-permute-done | bytes 1048608 | tf_op jit(solution)/shard_map/ppermute | solution.py:133
  326.8 3.9 multiply_convert_fusion.2
  330.7 3.7 fusion.23
  353.2 4.5 slice_reduce_fusion.1
  362.2 4.2 add_convert_fusion
  376.5 2.9 copy.145
  379.4 12.4 %collective-permute-done.23 = bf16[512,1024]{1,0:T(8,128)(2,1)} collective-permute-done((bf16[512,1024]{1,0:T(8,128)(2,1)}, bf16[512,1024]{1,0:T(8,128)(2,1)}, u32[]{:S(2)}, u32[]{:S(2)}) %collective-permute-start.23) | collective-permute-done | bytes 1048608 | tf_op jit(solution)/shard_map/ppermute | solution.py:133
  394.4 4.0 fusion.220
  398.5 8.6 %fusion.89 = bf16[1024,1024]{0,1:T(8,128)(2,1)} fusion(bf16[1024,1024]{1,0:T(8,128)(2,1)} %get-tuple-element.160, bf16[1024,1024]{1,0:T(8,128)(2,1)} %copy-done.112, bf16[1024,1024]{1,0:T(8,128)(2,1)S(1)} %copy-done.42, bf16[1024,1024]{1,0:T(8,128)(2,1)S(1)} %copy-done.40), kind=kOutput, calls=%fused_computation.203 | convolution fusion | flops 4312793088 | bytes 10485760 | tf_op jit(solution)/shard_map/ki,kj->ij/dot_general | solution.py:80
  410.0 3.5 fusion.127
  413.5 10.5 %multiply_reduce_fusion = (f32[4,1024]{1,0:T(4,128)S(1)}, f32[4,1024,1024]{1,2,0:T(8,128)}) fusion(f32[4,1024,1024]{1,2,0:T(8,128)S(1)} %bitcast.169, f32[4,1024]{1,0:T(4,128)S(1)} %log_add_fusion, bf16[1024,4,64]{0,2,1:T(8,128)(2,1)} %bitcast.185, bf16[1024,4,64]{0,2,1:T(8,128)(2,1)} %bitcast.187), kind=kOutput, calls=%fused_computation.1 | convolution fusion | flops 549449728 | bytes 34635776 | tf_op jit(solution)/shard_map/qhe,khe->hqk/dot_general | solution.py:62
  424.0 8.0 %multiply_convert_fusion = bf16[4,1024,1024]{1,2,0:T(8,128)(2,1)S(1)} fusion(f32[4,1024,1024]{1,2,0:T(8,128)} %get-tuple-element.163, f32[4,1024,1024]{1,2,0:T(8,128)S(1)} %bitcast.169, f32[4,1024]{1,0:T(4,128)S(1)} %get-tuple-element.162, f32[4,1024]{1,0:T(4,128)S(1)} %log_add_fusion), kind=kLoop, calls=%fused_computation | loop fusion | flops 16777216 | bytes 41975808 | tf_op jit(solution)/shard_map/convert_element_type | solution.py:65
  444.6 9.2 %fusion.94 = bf16[1024,1024]{0,1:T(8,128)(2,1)} fusion(bf16[1024,1024]{1,0:T(8,128)(2,1)} %copy-done.110, bf16[1024,1024]{1,0:T(8,128)(2,1)} %copy-done.109, bf16[512,1024]{1,0:T(8,128)(2,1)} %copy-done.105, bf16[512,1024]{1,0:T(8,128)(2,1)} %copy-done.71, bf16[512,1024]{1,0:T(8,128)(2,1)} %collective-permute-done.9, bf16[512,1024]{1,0:T(8,128)(2,1)S(1)} %copy-done.68), kind=kOutput, calls=%fused_computation.204 | convolution fusion | flops 4321181696 | bytes 10485760 | tf_op jit(solution)/shard_map/ki,kj->ij/dot_general | solution.py:80
  453.7 20.9 %all-reduce.4.cloned.1.call-done = f32[18,1024]{1,0:T(8,128)} async-done(((f32[18,1024]{1,0:T(8,128)}), f32[18,1024]{1,0:T(8,128)}) %all-reduce.4.cloned.1.call-update) | async-done | bytes 73744 | tf_op jit(solution)/shard_map/psum | solution.py:312
  474.9 4.1 pad_maximum_fusion
  479.0 6.5 copy.139
  505.2 8.0 %collective-permute-done.21 = bf16[1024,1,256]{2,0,1:T(8,128)(2,1)} collective-permute-done((bf16[1024,1,256]{2,0,1:T(8,128)(2,1)}, bf16[1024,1,256]{2,0,1:T(8,128)(2,1)}, u32[]{:S(2)}, u32[]{:S(2)}) %collective-permute-start.21) | collective-permute-done | bytes 524320 | tf_op jit(solution)/shard_map/ppermute | solution.py:133
  525.3 3.4 fusion.99
  544.1 3.8 all-reduce.6.cloned.1.call-done
  554.5 3.0 collective-permute-done.29
  562.2 14.6 %collective-permute-done.32 = bf16[128,1024]{0,1:T(8,128)(2,1)S(1)} collective-permute-done((bf16[128,1024]{0,1:T(8,128)(2,1)S(1)}, bf16[128,1024]{0,1:T(8,128)(2,1)S(1)}, u32[]{:S(2)}, u32[]{:S(2)}) %collective-permute-start.32) | collective-permute-done | bytes 262176 | tf_op jit(solution)/shard_map/ppermute | solution.py:124
  580.3 10.3 %collective-permute-done.33 = bf16[128,1024]{0,1:T(8,128)(2,1)S(1)} collective-permute-done((bf16[128,1024]{0,1:T(8,128)(2,1)S(1)}, bf16[128,1024]{0,1:T(8,128)(2,1)S(1)}, u32[]{:S(2)}, u32[]{:S(2)}) %collective-permute-start.33) | collective-permute-done | bytes 262176 | tf_op jit(solution)/shard_map/ppermute | solution.py:124
  595.8 51.2 %reduce-scatter.4.cloned.1.call-done = bf16[128,2048]{1,0:T(8,128)(2,1)} async-done(((bf16[1024,2048]{1,0:T(8,128)(2,1)}), bf16[128,2048]{1,0:T(8,128)(2,1)}) %reduce-scatter.4.cloned.1.call-update) | async-done | bytes 524304
  (480 shorter events, 194.2 us)
Async XLA Ops:
  7.2 20.7 %copy-start = (bf16[256,128]{1,0:T(8,128)(2,1)S(1)}, bf16[256,128]{1,0:T(8,128)(2,1)}, u32[]{:S(2)}) copy-start(bf16[256,128]{1,0:T(8,128)(2,1)} %param.30) | copy-start | bytes 196612
  7.2 171.8 %all-gather.2.cloned.1.call-start = ((), (), s32[]{:S(2)}) async-start(), calls=%async_computation.1 | async-start | bytes 4718592 | tf_op jit(solution)/shard_map/all_gather | solution.py:184
  8.7 18.3 %copy-start.97 = (s32[2,8]{1,0:T(2,128)S(1)}, s32[2,8]{1,0:T(2,128)}, u32[]{:S(2)}) copy-start(s32[2,8]{1,0:T(2,128)} %param.24) | copy-start | bytes 196
  8.7 18.3 %copy-start.96 = (s32[2,1024]{1,0:T(2,128)S(1)}, s32[2,1024]{1,0:T(2,128)}, u32[]{:S(2)}) copy-start(s32[2,1024]{1,0:T(2,128)} %param.23) | copy-start | bytes 24580
  8.7 19.0 %copy-start.98 = (bf16[128]{0:T(256)(128)(2,1)S(1)}, bf16[128]{0:T(256)(128)(2,1)}, u32[]{:S(2)}) copy-start(bf16[128]{0:T(256)(128)(2,1)} %param.32) | copy-start | bytes 772
  8.7 19.0 %copy-start.99 = (bf16[128]{0:T(256)(128)(2,1)S(1)}, bf16[128]{0:T(256)(128)(2,1)}, u32[]{:S(2)}) copy-start(bf16[128]{0:T(256)(128)(2,1)} %param.31) | copy-start | bytes 772
  9.1 77.5 %collective-permute-start = (bf16[128,1024]{0,1:T(8,128)(2,1)S(1)}, bf16[128,1024]{0,1:T(8,128)(2,1)}, u32[]{:S(2)}, u32[]{:S(2)}) collective-permute-start(bf16[128,1024]{0,1:T(8,128)(2,1)S(1)} %get-tuple-element.117), channel_id=1, source_target_pairs={{8,0},{16,8},{24,16},{28,24},{20,28},{12,20},{4,12},{0,4},{9,1},{1... | collective-permute-start | bytes 786440 | tf_op jit(solution)/shard_map/ppermute | solution.py:106
  12.1 74.5 %collective-permute-start.1 = (bf16[128,1024]{0,1:T(8,128)(2,1)S(1)}, bf16[128,1024]{0,1:T(8,128)(2,1)S(1)}, u32[]{:S(2)}, u32[]{:S(2)}) collective-permute-start(bf16[128,1024]{0,1:T(8,128)(2,1)S(1)} %get-tuple-element.117), channel_id=1, source_target_pairs={{0,8},{8,16},{16,24},{24,28},{28,20},{20,12},{12,4},{4,0},{1,9},{9... | collective-permute-start | bytes 786440 | tf_op jit(solution)/shard_map/ppermute | solution.py:104
  13.3 461.4 %all-reduce.4.cloned.1.call-start = ((), (), s32[]{:S(2)}) async-start(), calls=%async_computation.2 | async-start | bytes 196608 | tf_op jit(solution)/shard_map/psum | solution.py:312
  86.6 17.3 %collective-permute-start.2 = (bf16[128,1024]{0,1:T(8,128)(2,1)}, bf16[128,1024]{0,1:T(8,128)(2,1)}, u32[]{:S(2)}, u32[]{:S(2)}) collective-permute-start(bf16[128,1024]{0,1:T(8,128)(2,1)} %collective-permute-done), channel_id=1, source_target_pairs={{8,0},{16,8},{24,16},{28,24},{20,28},{12,20},{4,12},{0,4},{9,1},{1... | collective-permute-start | bytes 786440 | tf_op jit(solution)/shard_map/ppermute | solution.py:106
  86.6 15.8 %collective-permute-start.3 = (bf16[128,1024]{0,1:T(8,128)(2,1)S(1)}, bf16[128,1024]{0,1:T(8,128)(2,1)}, u32[]{:S(2)}, u32[]{:S(2)}) collective-permute-start(bf16[128,1024]{0,1:T(8,128)(2,1)S(1)} %collective-permute-done.1), channel_id=1, source_target_pairs={{0,8},{8,16},{16,24},{24,28},{28,20},{20,12},{12,4},{4,0},{1,9},{9... | collective-permute-start | bytes 786440 | tf_op jit(solution)/shard_map/ppermute | solution.py:104
  102.5 6.6 %collective-permute-start.5 = (bf16[128,1024]{0,1:T(8,128)(2,1)}, bf16[128,1024]{0,1:T(8,128)(2,1)S(1)}, u32[]{:S(2)}, u32[]{:S(2)}) collective-permute-start(bf16[128,1024]{0,1:T(8,128)(2,1)} %collective-permute-done.3), channel_id=1, source_target_pairs={{0,8},{8,16},{16,24},{24,28},{28,20},{20,12},{12,4},{4,0},{1,9},{9... | collective-permute-start | bytes 786440 | tf_op jit(solution)/shard_map/ppermute | solution.py:104
  103.9 6.9 %collective-permute-start.4 = (bf16[128,1024]{0,1:T(8,128)(2,1)}, bf16[128,1024]{0,1:T(8,128)(2,1)S(1)}, u32[]{:S(2)}, u32[]{:S(2)}) collective-permute-start(bf16[128,1024]{0,1:T(8,128)(2,1)} %collective-permute-done.2), channel_id=1, source_target_pairs={{8,0},{16,8},{24,16},{28,24},{20,28},{12,20},{4,12},{0,4},{9,1},{1... | collective-permute-start | bytes 786440 | tf_op jit(solution)/shard_map/ppermute | solution.py:106
  109.1 6.9 %collective-permute-start.6 = (bf16[128,1024]{0,1:T(8,128)(2,1)S(1)}, bf16[128,1024]{0,1:T(8,128)(2,1)S(1)}, u32[]{:S(2)}, u32[]{:S(2)}) collective-permute-start(bf16[128,1024]{0,1:T(8,128)(2,1)S(1)} %collective-permute-done.5), channel_id=1, source_target_pairs={{0,8},{8,16},{16,24},{24,28},{28,20},{20,12},{12,4},{4,0},{1,9},{9... | collective-permute-start | bytes 786440 | tf_op jit(solution)/shard_map/ppermute | solution.py:104
  116.1 25.7 %copy-start.13 = (bf16[1024,1024]{0,1:T(8,128)(2,1)}, bf16[1024,1024]{0,1:T(8,128)(2,1)S(1)}, u32[]{:S(2)}) copy-start(bf16[1024,1024]{0,1:T(8,128)(2,1)S(1)} %constant_dynamic-update-slice_fusion.1) | copy-start | bytes 6291460
  141.6 2.7 collective-permute-start.7
  141.7 28.3 %copy-start.6 = (f32[1024,1024]{1,0:T(8,128)S(1)}, f32[1024,1024]{1,0:T(8,128)}, u32[]{:S(2)}) copy-start(f32[1024,1024]{1,0:T(8,128)} %copy-done.5) | copy-start | bytes 12582916
  144.8 25.3 %collective-permute-start.8 = (bf16[512,1024]{1,0:T(8,128)(2,1)S(1)}, bf16[512,1024]{1,0:T(8,128)(2,1)S(1)}, u32[]{:S(2)}, u32[]{:S(2)}) collective-permute-start(bf16[512,1024]{1,0:T(8,128)(2,1)S(1)} %add_convert_fusion.5), channel_id=1, source_target_pairs={{0,2},{1,3},{2,0},{3,1},{4,6},{5,7},{6,4},{7,5},{8,10},{9,11},{10,... | collective-permute-start | bytes 3145736 | tf_op jit(solution)/shard_map/ppermute | solution.py:133
  171.2 7.8 %collective-permute-start.9 = (bf16[512,1024]{1,0:T(8,128)(2,1)S(1)}, bf16[512,1024]{1,0:T(8,128)(2,1)}, u32[]{:S(2)}, u32[]{:S(2)}) collective-permute-start(bf16[512,1024]{1,0:T(8,128)(2,1)S(1)} %multiply_convert_fusion.7), channel_id=1, source_target_pairs={{0,1},{1,0},{2,3},{3,2},{4,5},{5,4},{6,7},{7,6},{8,9},{9,8},{10,11... | collective-permute-start | bytes 3145736 | tf_op jit(solution)/shard_map/ppermute | solution.py:133
  188.8 2.7 collective-permute-start.17
  192.8 25.4 %collective-permute-start.18 = (bf16[512,1024]{1,0:T(8,128)(2,1)S(1)}, bf16[512,1024]{1,0:T(8,128)(2,1)}, u32[]{:S(2)}, u32[]{:S(2)}) collective-permute-start(bf16[512,1024]{1,0:T(8,128)(2,1)S(1)} %add_convert_fusion.1), channel_id=1, source_target_pairs={{0,2},{1,3},{2,0},{3,1},{4,6},{5,7},{6,4},{7,5},{8,10},{9,11},{10,... | collective-permute-start | bytes 3145736 | tf_op jit(solution)/shard_map/ppermute | solution.py:133
  220.4 18.2 %slice-start.4 = ((s8[16777216]{0:T(1024)(128)(4,1)}), s8[4194304]{0:T(1024)(128)(4,1)S(1)}, s32[]{:S(2)}) async-start(s8[16777216]{0:T(1024)(128)(4,1)} %bitcast.170), calls=%async_computation.9 | async-start | bytes 8388608
  220.4 18.2 %slice-start.5 = ((s8[16777216]{0:T(1024)(128)(4,1)}), s8[4194304]{0:T(1024)(128)(4,1)S(1)}, s32[]{:S(2)}) async-start(s8[16777216]{0:T(1024)(128)(4,1)} %bitcast.170), calls=%async_computation.10 | async-start | bytes 8388608
  223.9 2.7 collective-permute-start.19
  292.8 2.7 collective-permute-start.12
  295.9 25.3 %collective-permute-start.13 = (bf16[512,1024]{1,0:T(8,128)(2,1)S(1)}, bf16[512,1024]{1,0:T(8,128)(2,1)S(1)}, u32[]{:S(2)}, u32[]{:S(2)}) collective-permute-start(bf16[512,1024]{1,0:T(8,128)(2,1)S(1)} %add_convert_fusion.3), channel_id=1, source_target_pairs={{0,2},{1,3},{2,0},{3,1},{4,6},{5,7},{6,4},{7,5},{8,10},{9,11},{10,... | collective-permute-start | bytes 3145736 | tf_op jit(solution)/shard_map/ppermute | solution.py:133
  322.3 4.4 collective-permute-start.14
  336.7 25.1 %collective-permute-start.22 = (bf16[512,1024]{1,0:T(8,128)(2,1)}, bf16[512,1024]{1,0:T(8,128)(2,1)}, u32[]{:S(2)}, u32[]{:S(2)}) collective-permute-start(bf16[512,1024]{1,0:T(8,128)(2,1)} %convolution_convert_fusion.2), channel_id=1, source_target_pairs={{0,1},{1,0},{2,3},{3,2},{4,5},{5,4},{6,7},{7,6},{8,9},{9,8},{10,11... | collective-permute-start | bytes 3145736 | tf_op jit(solution)/shard_map/ppermute | solution.py:133
  347.3 138.3 %collective-permute-start.10 = (bf16[1024,2,256]{2,0,1:T(8,128)(2,1)}, bf16[1024,2,256]{2,0,1:T(8,128)(2,1)}, u32[]{:S(2)}, u32[]{:S(2)}) collective-permute-start(bf16[1024,2,256]{2,0,1:T(8,128)(2,1)} %fusion.154), channel_id=1, source_target_pairs={{0,1},{1,0},{2,3},{3,2},{4,5},{5,4},{6,7},{7,6},{8,9},{9,8},{10,11... | collective-permute-start | bytes 3145736 | tf_op jit(solution)/shard_map/ppermute | solution.py:133
  366.4 25.4 %collective-permute-start.23 = (bf16[512,1024]{1,0:T(8,128)(2,1)}, bf16[512,1024]{1,0:T(8,128)(2,1)}, u32[]{:S(2)}, u32[]{:S(2)}) collective-permute-start(bf16[512,1024]{1,0:T(8,128)(2,1)} %add_convert_fusion), channel_id=1, source_target_pairs={{0,2},{1,3},{2,0},{3,1},{4,6},{5,7},{6,4},{7,5},{8,10},{9,11},{10,... | collective-permute-start | bytes 3145736 | tf_op jit(solution)/shard_map/ppermute | solution.py:133
  370.5 118.3 %collective-permute-start.20 = (bf16[1024,2,256]{2,0,1:T(8,128)(2,1)}, bf16[1024,2,256]{2,0,1:T(8,128)(2,1)}, u32[]{:S(2)}, u32[]{:S(2)}) collective-permute-start(bf16[1024,2,256]{2,0,1:T(8,128)(2,1)} %dynamic-slice_bitcast_fusion.1), channel_id=1, source_target_pairs={{0,1},{1,0},{2,3},{3,2},{4,5},{5,4},{6,7},{7,6},{8,9},{9,8},{10,11... | collective-permute-start | bytes 3145736 | tf_op jit(solution)/shard_map/ppermute | solution.py:133
  398.5 8.7 %collective-permute-start.24 = (bf16[512,1024]{1,0:T(8,128)(2,1)S(1)}, bf16[512,1024]{1,0:T(8,128)(2,1)}, u32[]{:S(2)}, u32[]{:S(2)}) collective-permute-start(bf16[512,1024]{1,0:T(8,128)(2,1)S(1)} %get-tuple-element.71), channel_id=1, source_target_pairs={{0,1},{1,0},{2,3},{3,2},{4,5},{5,4},{6,7},{7,6},{8,9},{9,8},{10,11... | collective-permute-start | bytes 3145736 | tf_op jit(solution)/shard_map/ppermute | solution.py:133
  444.5 30.4 %copy-start.61 = (bf16[1024,1024]{0,1:T(8,128)(2,1)S(1)}, bf16[1024,1024]{0,1:T(8,128)(2,1)}, u32[]{:S(2)}) copy-start(bf16[1024,1024]{0,1:T(8,128)(2,1)} %fusion.89) | copy-start | bytes 6291460
  444.5 103.3 %all-reduce.6.cloned.1.call-start = ((), (), s32[]{:S(2)}) async-start(), calls=%async_computation.3 | async-start | bytes 196608 | tf_op jit(solution)/shard_map/psum | solution.py:312
  474.7 172.3 %reduce-scatter.4.cloned.1.call-start = ((), (), s32[]{:S(2)}) async-start(), calls=%async_computation.4 | async-start | bytes 4718592
  488.7 12.7 %collective-permute-start.11 = (bf16[1024,1,256]{2,0,1:T(8,128)(2,1)}, bf16[1024,1,256]{2,0,1:T(8,128)(2,1)}, u32[]{:S(2)}, u32[]{:S(2)}) collective-permute-start(bf16[1024,1,256]{2,0,1:T(8,128)(2,1)} %dynamic-slice_convert_fusion.3), channel_id=1, source_target_pairs={{0,2},{1,3},{2,0},{3,1},{4,6},{5,7},{6,4},{7,5},{8,10},{9,11},{10,... | collective-permute-start | bytes 1572872 | tf_op jit(solution)/shard_map/ppermute | solution.py:133
  496.5 22.1 %collective-permute-start.15 = (bf16[1024,2,256]{2,0,1:T(8,128)(2,1)}, bf16[1024,2,256]{2,0,1:T(8,128)(2,1)S(1)}, u32[]{:S(2)}, u32[]{:S(2)}) collective-permute-start(bf16[1024,2,256]{2,0,1:T(8,128)(2,1)} %fusion.150), channel_id=1, source_target_pairs={{0,1},{1,0},{2,3},{3,2},{4,5},{5,4},{6,7},{7,6},{8,9},{9,8},{10,11... | collective-permute-start | bytes 3145736 | tf_op jit(solution)/shard_map/ppermute | solution.py:133
  498.6 14.7 %collective-permute-start.21 = (bf16[1024,1,256]{2,0,1:T(8,128)(2,1)}, bf16[1024,1,256]{2,0,1:T(8,128)(2,1)}, u32[]{:S(2)}, u32[]{:S(2)}) collective-permute-start(bf16[1024,1,256]{2,0,1:T(8,128)(2,1)} %dynamic-slice_convert_fusion.1), channel_id=1, source_target_pairs={{0,2},{1,3},{2,0},{3,1},{4,6},{5,7},{6,4},{7,5},{8,10},{9,11},{10,... | collective-permute-start | bytes 1572872 | tf_op jit(solution)/shard_map/ppermute | solution.py:133
  519.9 33.4 %collective-permute-start.16 = (bf16[1024,1,256]{2,0,1:T(8,128)(2,1)}, bf16[1024,1,256]{2,0,1:T(8,128)(2,1)}, u32[]{:S(2)}, u32[]{:S(2)}) collective-permute-start(bf16[1024,1,256]{2,0,1:T(8,128)(2,1)} %dynamic-slice_convert_fusion.2), channel_id=1, source_target_pairs={{0,2},{1,3},{2,0},{3,1},{4,6},{5,7},{6,4},{7,5},{8,10},{9,11},{10,... | collective-permute-start | bytes 1572872 | tf_op jit(solution)/shard_map/ppermute | solution.py:133
  529.6 8.3 %collective-permute-start.27 = (bf16[128,1024]{0,1:T(8,128)(2,1)}, bf16[128,1024]{0,1:T(8,128)(2,1)}, u32[]{:S(2)}, u32[]{:S(2)}) collective-permute-start(bf16[128,1024]{0,1:T(8,128)(2,1)} %get-tuple-element.89), channel_id=1, source_target_pairs={{0,8},{8,16},{16,24},{24,28},{28,20},{20,12},{12,4},{4,0},{1,9},{9... | collective-permute-start | bytes 786440 | tf_op jit(solution)/shard_map/ppermute | solution.py:124
  531.2 23.3 %collective-permute-start.31 = (bf16[128,1024]{0,1:T(8,128)(2,1)}, bf16[128,1024]{0,1:T(8,128)(2,1)S(1)}, u32[]{:S(2)}, u32[]{:S(2)}) collective-permute-start(bf16[128,1024]{0,1:T(8,128)(2,1)} %get-tuple-element.90), channel_id=1, source_target_pairs={{8,0},{16,8},{24,16},{28,24},{20,28},{12,20},{4,12},{0,4},{9,1},{1... | collective-permute-start | bytes 786440 | tf_op jit(solution)/shard_map/ppermute | solution.py:124
  539.7 10.0 %collective-permute-start.28 = (bf16[128,1024]{0,1:T(8,128)(2,1)}, bf16[128,1024]{0,1:T(8,128)(2,1)}, u32[]{:S(2)}, u32[]{:S(2)}) collective-permute-start(bf16[128,1024]{0,1:T(8,128)(2,1)} %add_convert_fusion.12), channel_id=1, source_target_pairs={{0,8},{8,16},{16,24},{24,28},{28,20},{20,12},{12,4},{4,0},{1,9},{9... | collective-permute-start | bytes 786440 | tf_op jit(solution)/shard_map/ppermute | solution.py:124
  544.1 32.8 %collective-permute-start.25 = (bf16[1024,2,256]{2,0,1:T(8,128)(2,1)}, bf16[1024,2,256]{2,0,1:T(8,128)(2,1)S(1)}, u32[]{:S(2)}, u32[]{:S(2)}) collective-permute-start(bf16[1024,2,256]{2,0,1:T(8,128)(2,1)} %dynamic-slice_bitcast_fusion), channel_id=1, source_target_pairs={{0,1},{1,0},{2,3},{3,2},{4,5},{5,4},{6,7},{7,6},{8,9},{9,8},{10,11... | collective-permute-start | bytes 3145736 | tf_op jit(solution)/shard_map/ppermute | solution.py:133
  550.8 6.7 %collective-permute-start.29 = (bf16[128,1024]{0,1:T(8,128)(2,1)S(1)}, bf16[128,1024]{0,1:T(8,128)(2,1)S(1)}, u32[]{:S(2)}, u32[]{:S(2)}) collective-permute-start(bf16[128,1024]{0,1:T(8,128)(2,1)S(1)} %add_convert_fusion.11), channel_id=1, source_target_pairs={{0,8},{8,16},{16,24},{24,28},{28,20},{20,12},{12,4},{4,0},{1,9},{9... | collective-permute-start | bytes 786440 | tf_op jit(solution)/shard_map/ppermute | solution.py:124
  557.6 19.1 %collective-permute-start.32 = (bf16[128,1024]{0,1:T(8,128)(2,1)S(1)}, bf16[128,1024]{0,1:T(8,128)(2,1)S(1)}, u32[]{:S(2)}, u32[]{:S(2)}) collective-permute-start(bf16[128,1024]{0,1:T(8,128)(2,1)S(1)} %get-tuple-element.88), channel_id=1, source_target_pairs={{8,0},{16,8},{24,16},{28,24},{20,28},{12,20},{4,12},{0,4},{9,1},{1... | collective-permute-start | bytes 786440 | tf_op jit(solution)/shard_map/ppermute | solution.py:124
  561.0 19.3 %collective-permute-start.30 = (bf16[128,1024]{0,1:T(8,128)(2,1)S(1)}, bf16[128,1024]{0,1:T(8,128)(2,1)S(1)}, u32[]{:S(2)}, u32[]{:S(2)}) collective-permute-start(bf16[128,1024]{0,1:T(8,128)(2,1)S(1)} %get-tuple-element.87), channel_id=1, source_target_pairs={{0,8},{8,16},{16,24},{24,28},{28,20},{20,12},{12,4},{4,0},{1,9},{9... | collective-permute-start | bytes 786440 | tf_op jit(solution)/shard_map/ppermute | solution.py:124
  576.9 13.8 %collective-permute-start.33 = (bf16[128,1024]{0,1:T(8,128)(2,1)S(1)}, bf16[128,1024]{0,1:T(8,128)(2,1)S(1)}, u32[]{:S(2)}, u32[]{:S(2)}) collective-permute-start(bf16[128,1024]{0,1:T(8,128)(2,1)S(1)} %add_convert_fusion.8), channel_id=1, source_target_pairs={{8,0},{16,8},{24,16},{28,24},{20,28},{12,20},{4,12},{0,4},{9,1},{1... | collective-permute-start | bytes 786440 | tf_op jit(solution)/shard_map/ppermute | solution.py:124
  578.8 13.6 %collective-permute-start.26 = (bf16[1024,1,256]{2,0,1:T(8,128)(2,1)S(1)}, bf16[1024,1,256]{2,0,1:T(8,128)(2,1)S(1)}, u32[]{:S(2)}, u32[]{:S(2)}) collective-permute-start(bf16[1024,1,256]{2,0,1:T(8,128)(2,1)S(1)} %dynamic-slice_convert_fusion), channel_id=1, source_target_pairs={{0,2},{1,3},{2,0},{3,1},{4,6},{5,7},{6,4},{7,5},{8,10},{9,11},{10,... | collective-permute-start | bytes 1572872 | tf_op jit(solution)/shard_map/ppermute | solution.py:133
  (112 other events, 595.1 us)
Sparse Core Ops, SparseCore 0:
  13.4 80.5 all-gather.1
  444.6 29.9 all-reduce.3
  478.4 69.3 all-reduce.5
  551.8 95.1 reduce-scatter.3
